TPU v7x, 32 devices: a whole 2x2x4 slice. The times are simulated.
32 devices in a mesh: rep: 4 (over z), px: 4 (over x, core), py: 2 (over y).
Axes of the slice: x: 2, y: 2, z: 4, core: 2. Of those that a mesh axis runs over, the one named last changes fastest.
Arguments:
- state: float32 [12, 2, 192, 96, 256], P('rep', None, 'px', 'py'), parts along dimension 0, may hold values from -6 to 6
- cotangent: float32 [12, 2, 192, 96, 256], P('rep', None, 'px', 'py'), parts along dimension 0, may hold values from -6 to 6
- w_in: bfloat16 [512, 192], replicated, may hold values from -0.4375 to 0.4375
- b_in: float32 [512], replicated, may hold values from -5 to 5
- w_out: bfloat16 [192, 512], replicated, may hold values from -0.25 to 0.25
Outputs:
- state_grad: float32 [12, 2, 192, 96, 256], P('rep', None, 'px', 'py'), parts along dimension 0
- grad_in: float32 [512, 768], P(('px', 'py'), 'rep'), parts along dimension 1
- grad_out: float32 [768, 512], P('rep', ('px', 'py')), parts along dimension 0
- grad_bias: float32 [4, 512], P('rep', ('px', 'py')), parts along dimension 0
There are 4 independent parts, one for each index of `rep`. A program takes and returns all parts, laid end to end along the dimension named above; an argument that names none is the same for every part. Nothing has to cross between parts.
All inputs are finite; a program needn't handle non-finite values.
Results may differ from a plain program's by a relative error of at most 0.0065.
The roundings to bfloat16 on the way count: a program that leaves them out, or rounds other values in their place, can miss the bound.
Values may be sent and summed in bfloat16 or wider, within the bound.
A program may use at most 448 MiB of HBM per device.

v0:
```python
import math
import jax
import jax.numpy as jnp
from jax import lax
from jax.sharding import PartitionSpec as P

PATCH = 4
NU_DT = 5e-05
TIME_STEP = 0.01
FORCING = 20.0


def angles(leading, trailing, length):
    product = leading[:, None] * trailing[None, :] % length
    phases = product.astype(jnp.float32) * (2.0 * math.pi / length)
    factor = 1.0 / math.sqrt(length)
    return (jnp.cos(phases) * factor, jnp.sin(phases) * factor)


def mode_ids(count, length):
    counter = jnp.arange(count, dtype=jnp.int32)
    return jnp.where(counter < count // 2, counter, counter + length - count)


def mode_table(modes, length, direction):
    cosine, sine_part = angles(modes, jnp.arange(length, dtype=jnp.int32), length)
    top_rows = jnp.stack([cosine, direction * sine_part], axis=1)
    low_rows = jnp.stack([-direction * sine_part, cosine], axis=1)
    return jnp.stack([top_rows, low_rows], axis=0).astype(jnp.bfloat16)


def complex_table(length, direction):
    return mode_table(jnp.arange(length, dtype=jnp.int32), length, direction)


def real_table(length, mode_count):
    cosine, sine_part = angles(
        jnp.arange(mode_count, dtype=jnp.int32), jnp.arange(length, dtype=jnp.int32), length
    )
    return jnp.stack([cosine, -sine_part], axis=0).astype(jnp.bfloat16)


def box_order(length, span):
    counter = jnp.arange(length, dtype=jnp.int32)
    local = counter % span
    rows = span // PATCH
    return counter - local + local % rows * PATCH + local // rows


def signed(counter, length):
    return jnp.where(counter < length // 2, counter, counter - length).astype(jnp.float32)


def factors(ky_ids, kz_ids, length, ky_count):
    cutoff = length // 3
    wave_y = signed(ky_ids, ky_count)[:, None, None]
    wave_z = kz_ids.astype(jnp.float32)[None, :, None]
    wave_x = signed(jnp.arange(length, dtype=jnp.int32), length)[None, None, :]
    retained = (
        (jnp.abs(wave_x) <= cutoff) & (jnp.abs(wave_y) <= cutoff) & (wave_z <= cutoff)
    ).astype(jnp.float32)
    square = wave_x * wave_x + wave_y * wave_y + wave_z * wave_z
    damping = jnp.exp(-NU_DT * square)
    weight = jnp.where(kz_ids[None, :, None] == 0, 1.0, 2.0).astype(jnp.float32)
    return ((wave_x, wave_y, wave_z), retained, damping, weight, square)


def cross(former, latter):
    return [
        former[1] * latter[2] - former[2] * latter[1],
        former[2] * latter[0] - former[0] * latter[2],
        former[0] * latter[1] - former[1] * latter[0],
    ]


def curl_modes(waves, spectra):
    real_part = cross(waves, [spectra[slot, 0] for slot in range(3)])
    imag_part = cross(waves, [spectra[slot, 1] for slot in range(3)])
    return jnp.stack([jnp.stack([-imag_part[slot], real_part[slot]]) for slot in range(3)])


def project(waves, square, spectra):
    dotted = waves[0] * spectra[0] + waves[1] * spectra[1] + waves[2] * spectra[2]
    along_k = dotted / jnp.maximum(square, 1.0)
    return jnp.stack([spectra[slot] - waves[slot] * along_k for slot in range(3)])


def to_physical(spectra):
    channels, paired, width_y, width_z, length = spectra.shape
    parts_x = lax.axis_size("px")
    parts_y = lax.axis_size("py")
    order_y = box_order(length, length)
    order_z = box_order(length, length)
    inverse = complex_table(length, 1.0)
    y_table = mode_table(mode_ids(width_y * parts_x, length), length, 1.0)[..., order_y].reshape(
        2, parts_x, width_y, 2, length
    )
    z_table = real_table(length, width_z * parts_y)[..., order_z].reshape(
        2, parts_y, width_z, length
    )
    flat = spectra.astype(jnp.bfloat16).reshape(channels, paired, width_y * width_z, length)
    along_x = jnp.einsum(
        "crpn,rnsx->csxp", flat, inverse, preferred_element_type=jnp.float32
    ).astype(jnp.bfloat16)
    along_x = along_x.reshape(channels, 2, length, 1, width_y * width_z)
    moved = lax.all_to_all(along_x, ("px", "py"), split_axis=2, concat_axis=3, tiled=True)
    blocks = moved.reshape(moved.shape[0], 2, moved.shape[2], parts_x, parts_y, width_y, width_z)
    along_y = jnp.einsum(
        "csxjlam,sjaty->cxtlmy", blocks, y_table, preferred_element_type=jnp.float32
    ).astype(jnp.bfloat16)
    return jnp.einsum(
        "cxtlmy,tlmz->cxyz", along_y, z_table, preferred_element_type=jnp.float32
    ).astype(jnp.bfloat16)


def to_spectral(field, ky_count, mode_count):
    channels, span_x, span_y, length = field.shape
    parts_x = lax.axis_size("px")
    parts_y = lax.axis_size("py")
    width_y = ky_count // parts_x
    width_z = mode_count // parts_y
    order_y = box_order(length, span_y)
    order_z = box_order(length, length)
    forward = complex_table(length, -1.0)
    y_table = (
        mode_table(mode_ids(ky_count, length), length, -1.0)
        .transpose(0, 3, 2, 1)[:, order_y]
        .reshape(2, length, 2, parts_x, width_y)
    )
    z_table = real_table(length, mode_count)[..., order_z].reshape(2, parts_y, width_z, length)
    along_z = jnp.einsum(
        "cxyz,rlmz->crlmxy", field, z_table, preferred_element_type=jnp.float32
    ).astype(jnp.bfloat16)
    along_y = jnp.einsum(
        "crlmxy,rysja->csxjlam", along_z, y_table, preferred_element_type=jnp.float32
    ).astype(jnp.bfloat16)
    along_y = along_y.reshape(channels, 2, span_x, parts_x * parts_y, width_y * width_z)
    moved = lax.all_to_all(along_y, ("px", "py"), split_axis=3, concat_axis=2, tiled=True)
    number = moved.shape[0]
    flat = moved.reshape(number, 2, length, -1)
    along_x = jnp.einsum("csxp,sxtn->ctpn", flat, forward, preferred_element_type=jnp.float32)
    return along_x.reshape(number, 2, width_y, width_z, length)


def to_boxes(field):
    channels, span_x, span_y, span_z = field.shape
    tiles = field.reshape(
        channels, span_x // PATCH, PATCH, PATCH, span_y // PATCH, PATCH, span_z // PATCH
    )
    return tiles.transpose(0, 2, 3, 5, 1, 4, 6).reshape(channels * PATCH**3, -1)


def from_boxes(box_values, layout):
    channels, span_x, span_y, span_z = layout
    tiles = box_values.reshape(
        channels, PATCH, PATCH, PATCH, span_x // PATCH, span_y // PATCH, span_z // PATCH
    )
    return tiles.transpose(0, 4, 1, 2, 5, 3, 6).reshape(layout)


def closure_terms(velocity, force_adj, w_in, b_in, w_out):
    features = to_boxes(velocity)
    adjoints = to_boxes(force_adj)
    pre_act = jnp.dot(w_in, features, preferred_element_type=jnp.float32) + b_in[:, None]
    hidden = jax.nn.silu(pre_act).astype(jnp.bfloat16)
    sigmoid = jax.nn.sigmoid(pre_act)
    hidden_adj = FORCING * jnp.dot(w_out.T, adjoints, preferred_element_type=jnp.float32)
    pre_adj = (hidden_adj * sigmoid * (1.0 + pre_act * (1.0 - sigmoid))).astype(jnp.bfloat16)
    grad_in = jnp.dot(pre_adj, features.T, preferred_element_type=jnp.float32)
    grad_out = FORCING * jnp.dot(adjoints, hidden.T, preferred_element_type=jnp.float32)
    grad_bias = jnp.sum(pre_adj.astype(jnp.float32), axis=1)[None, :]
    feat_adj = jnp.dot(w_in.T, pre_adj, preferred_element_type=jnp.float32).astype(jnp.bfloat16)
    feat_adj = lax.optimization_barrier(from_boxes(feat_adj, velocity.shape))
    return (feat_adj, grad_in, grad_out, grad_bias)


def field_cross(former, latter):
    return cross(
        [former[slot].astype(jnp.float32) for slot in range(3)],
        [latter[slot].astype(jnp.float32) for slot in range(3)],
    )


def shards(state, cotangent, w_in, b_in, w_out):
    width_y = state.shape[2]
    width_z = state.shape[3]
    length = state.shape[4]
    ky_count = width_y * lax.axis_size("px")
    ky_ids = lax.axis_index("px") * width_y + jnp.arange(width_y, dtype=jnp.int32)
    kz_ids = lax.axis_index("py") * width_z + jnp.arange(width_z, dtype=jnp.int32)
    waves, retained, damping, weight, square = factors(ky_ids, kz_ids, length, ky_count)
    kept = retained * state
    force_spec = TIME_STEP * retained * project(waves, square, damping * cotangent)
    modes = width_z * lax.axis_size("py")
    force_adj = to_physical(force_spec)
    velocity = to_physical(weight * kept)
    vorticity = to_physical(weight * curl_modes(waves, kept))
    vort_adj = jnp.stack(field_cross(force_adj, velocity)).astype(jnp.bfloat16)
    spec_vort = to_spectral(vort_adj, ky_count, modes)
    feat_adj, grad_in, grad_out, grad_bias = closure_terms(velocity, force_adj, w_in, b_in, w_out)
    turned = field_cross(vorticity, force_adj)
    vel_adj = jnp.stack([feat_adj[slot].astype(jnp.float32) + turned[slot] for slot in range(3)])
    spec_vel = to_spectral(vel_adj.astype(jnp.bfloat16), ky_count, modes)
    state_grad = damping * cotangent + weight * retained * (spec_vel + curl_modes(waves, spec_vort))
    grad_in, grad_out, grad_bias = (
        lax.psum_scatter(grad_in, ("px", "py"), scatter_dimension=0, tiled=True),
        lax.psum_scatter(grad_out, ("px", "py"), scatter_dimension=1, tiled=True),
        lax.psum_scatter(grad_bias, ("px", "py"), scatter_dimension=1, tiled=True),
    )
    return (state_grad, grad_in, grad_out, grad_bias)


def solution(mesh):
    return jax.shard_map(
        shards,
        mesh=mesh,
        in_specs=(
            P("rep", None, "px", "py", None),
            P("rep", None, "px", "py", None),
            P(),
            P(),
            P(),
        ),
        out_specs=(
            P("rep", None, "px", "py", None),
            P(("px", "py"), "rep"),
            P("rep", ("px", "py")),
            P("rep", ("px", "py")),
        ),
        check_vma=False,
    )
```

profile of v0, /device:TPU:0, one launch (start us, length us, event | category | flops | bytes accessed | tf_op | source)
XLA Modules:
  0.0 1128.6 jit_solution(6317094853116231177)
XLA Ops:
  46.3 23.6 %copy.174 = bf16[3,2,256,1,2304]{4,1,3,0,2:T(2,128)(2,1)} copy(bf16[3,2,256,1,2304]{4,2,0,1,3:T(8,128)(2,1)S(1)} %fusion.75) | data formatting | bytes 14155776 | tf_op jit(solution)/shard_map/reshape | solution.py:105
  69.9 16.6 %all-to-all-start = ((bf16[3,2,256,1,2304]{4,1,3,0,2:T(2,128)(2,1)}), bf16[3,2,256,1,2304]{4,1,3,0,2:T(2,128)(2,1)}, u32[]{:S(2)}, u32[]{:S(2)}) async-start(bf16[3,2,256,1,2304]{4,1,3,0,2:T(2,128)(2,1)} %copy.174), calls=%async_computation | async-start | bytes 14155776 | tf_op jit(solution)/shard_map/all_to_all | solution.py:106
  105.6 27.6 %copy.180 = bf16[3,2,256,1,2304]{4,1,3,0,2:T(2,128)(2,1)} copy(bf16[3,2,256,1,2304]{4,2,0,1,3:T(8,128)(2,1)} %fusion.74) | data formatting | bytes 14155776 | tf_op jit(solution)/shard_map/reshape | solution.py:105
  133.2 33.0 %all-to-all-done = bf16[3,2,256,1,2304]{4,1,3,0,2:T(2,128)(2,1)} async-done(((bf16[3,2,256,1,2304]{4,1,3,0,2:T(2,128)(2,1)}), bf16[3,2,256,1,2304]{4,1,3,0,2:T(2,128)(2,1)}, u32[]{:S(2)}, u32[]{:S(2)}) %all-to-all-start) | async-done | bytes 7077920 | tf_op jit(solution)/shard_map/all_to_all | solution.py:106
  204.4 24.0 %copy.187 = bf16[3,2,256,1,2304]{4,1,3,0,2:T(2,128)(2,1)} copy(bf16[3,2,256,1,2304]{4,2,0,1,3:T(8,128)(2,1)S(1)} %fusion.78) | data formatting | bytes 14155776 | tf_op jit(solution)/shard_map/reshape | solution.py:105
  240.1 28.9 %reshape.1131 = bf16[3,2,32,4,2,48,48]{6,5,4,3,2,1,0:T(8,128)(2,1)} reshape(bf16[3,2,32,8,1,2304]{5,3,2,1,0,4:T(8,128)(2,1)} %bitcast.414) | data formatting | bytes 14155776 | tf_op jit(solution)/shard_map/reshape | solution.py:107
  283.7 29.0 %reshape.1136 = bf16[3,2,32,4,2,48,48]{6,5,4,3,2,1,0:T(8,128)(2,1)} reshape(bf16[3,2,32,8,1,2304]{5,3,2,1,0,4:T(8,128)(2,1)} %bitcast.415) | data formatting | bytes 14155776 | tf_op jit(solution)/shard_map/reshape | solution.py:107
  312.7 16.2 %bitcast_convert_fusion.3 = bf16[3,32,256,256]{3,2,1,0:T(8,128)(2,1)} fusion(bf16[2,4,48,2,256,1,1,1]{4,2,1,3,0,7,6,5:T(8,128)(2,1)S(1)} %bitcast.429, bf16[2,2,48,256,1,1]{3,2,1,0,5,4:T(8,128)(2,1)S(1)} %bitcast.432, bf16[3,2,32,4,2,48,48]{6,5,4,3,2,1,0:T(8,128)(2,1)} %reshape.1136), kind=kOutput, calls=%fused_computation.21 | convolution fusion | flops 6050807808 | bytes 20152320 | tf_op jit(solution)/shard_map/cxtlmy,tlmz->cxyz/dot_general | solution.py:111
  328.9 36.2 %reshape.1137 = bf16[3,8,4,4,64,4,64]{6,5,4,3,2,1,0:T(4,128)(2,1)} reshape(bf16[3,32,256,256]{3,2,1,0:T(8,128)(2,1)} %bitcast_convert_fusion.3) | data formatting | bytes 25165824 | tf_op jit(solution)/shard_map/reshape | solution.py:147
  365.0 16.4 %bitcast_convert_fusion.4 = bf16[3,32,256,256]{3,2,1,0:T(8,128)(2,1)} fusion(bf16[2,4,48,2,256,1,1,1]{4,2,1,3,0,7,6,5:T(8,128)(2,1)S(1)} %bitcast.430, bf16[2,2,48,256,1,1]{3,2,1,0,5,4:T(8,128)(2,1)S(1)} %bitcast.433, bf16[3,2,32,4,2,48,48]{6,5,4,3,2,1,0:T(8,128)(2,1)} %reshape.1131), kind=kOutput, calls=%fused_computation.22 | convolution fusion | flops 6050807808 | bytes 20152320 | tf_op jit(solution)/shard_map/cxtlmy,tlmz->cxyz/dot_general | solution.py:111
  381.4 36.2 %reshape.1132 = bf16[3,8,4,4,64,4,64]{6,5,4,3,2,1,0:T(4,128)(2,1)} reshape(bf16[3,32,256,256]{3,2,1,0:T(8,128)(2,1)} %bitcast_convert_fusion.4) | data formatting | bytes 25165824 | tf_op jit(solution)/shard_map/reshape | solution.py:147
  435.4 15.6 %fusion.11 = bf16[3,2,32,4,2,48,48]{6,5,2,4,0,3,1:T(8,128)(2,1)} fusion(bf16[2,2,48,3,32,256]{5,2,0,4,1,3:T(8,128)(2,1)} %fusion.27, bf16[2,256,2,4,48,1,1,1]{1,4,3,2,0,7,6,5:T(8,128)(2,1)} %bitcast.427), kind=kOutput, calls=%fused_computation.27 | convolution fusion | flops 3627417600 | bytes 16908288 | tf_op jit(solution)/shard_map/crlmxy,rysja->csxjlam/dot_general | solution.py:134
  451.0 18.1 %copy.270 = bf16[3,2,32,4,2,48,48]{6,5,2,1,0,4,3:T(8,128)(2,1)} copy(bf16[3,2,32,4,2,48,48]{6,5,2,4,0,3,1:T(8,128)(2,1)} %fusion.11) | data formatting | bytes 14155776 | tf_op jit(solution)/shard_map/reshape | solution.py:137
  469.1 26.4 %reshape.1212 = bf16[3,2,32,8,2304]{4,2,1,0,3:T(8,128)(2,1)} reshape(bf16[3,2,32,4,2,48,48]{6,5,2,1,0,4,3:T(8,128)(2,1)} %copy.270) | data formatting | bytes 14155776 | tf_op jit(solution)/shard_map/reshape | solution.py:137
  495.5 22.6 %copy.327 = bf16[3,8,4,4,64,4,64]{6,4,1,5,3,2,0:T(8,128)(2,1)} copy(bf16[3,8,4,4,64,4,64]{6,5,4,3,2,1,0:T(4,128)(2,1)} %reshape.1137) | data formatting | bytes 25165824 | tf_op jit(solution)/shard_map/reshape | solution.py:147
  518.2 29.1 %reshape.1138 = bf16[192,32768]{1,0:T(8,128)(2,1)} reshape(bf16[3,4,4,4,8,64,64]{6,5,4,3,2,1,0:T(8,128)(2,1)} %bitcast.405) | data formatting | bytes 25165824 | tf_op jit(solution)/shard_map/reshape | solution.py:150
  562.0 29.2 %reshape.1142 = bf16[3,2,32,4,2,48,48]{6,5,4,3,2,1,0:T(8,128)(2,1)} reshape(bf16[3,2,32,8,1,2304]{5,3,2,1,0,4:T(8,128)(2,1)} %bitcast.416) | data formatting | bytes 14155776 | tf_op jit(solution)/shard_map/reshape | solution.py:107
  591.1 16.2 %bitcast_convert_fusion.2 = bf16[3,32,256,256]{3,2,1,0:T(8,128)(2,1)} fusion(bf16[2,4,48,2,256,1,1,1]{4,2,1,3,0,7,6,5:T(8,128)(2,1)S(1)} %bitcast.431, bf16[2,2,48,256,1,1]{3,2,1,0,5,4:T(8,128)(2,1)S(1)} %bitcast.435, bf16[3,2,32,4,2,48,48]{6,5,4,3,2,1,0:T(8,128)(2,1)} %reshape.1142), kind=kOutput, calls=%fused_computation.20 | convolution fusion | flops 6050807808 | bytes 20152320 | tf_op jit(solution)/shard_map/cxtlmy,tlmz->cxyz/dot_general | solution.py:111
  607.3 22.6 %copy.328 = bf16[3,8,4,4,64,4,64]{6,4,1,5,3,2,0:T(8,128)(2,1)} copy(bf16[3,8,4,4,64,4,64]{6,5,4,3,2,1,0:T(4,128)(2,1)} %reshape.1132) | data formatting | bytes 25165824 | tf_op jit(solution)/shard_map/reshape | solution.py:147
  629.9 29.1 %reshape.1133 = bf16[192,32768]{1,0:T(8,128)(2,1)} reshape(bf16[3,4,4,4,8,64,64]{6,5,4,3,2,1,0:T(8,128)(2,1)} %bitcast.406) | data formatting | bytes 25165824 | tf_op jit(solution)/shard_map/reshape | solution.py:150
  659.0 27.8 %fusion.156 = f32[32768,512]{1,0:T(8,128)} fusion(bf16[192,32768]{1,0:T(8,128)(2,1)} %reshape.1138, bf16[512,192]{0,1:T(8,128)(2,1)S(1)} %copy-done), kind=kOutput, calls=%fused_computation.263 | convolution fusion | flops 6442450944 | bytes 79888384 | tf_op jit(solution)/shard_map/dot_general | solution.py:164
  686.8 46.9 %convert_reduce_fusion = (f32[512]{0:T(512)S(1)}, bf16[512,32768]{0,1:T(8,128)(2,1)}) fusion(f32[32768,512]{1,0:T(8,128)} %fusion.156, f32[512]{0:T(512)S(1)} %copy-done.32, bf16[192,32768]{1,0:T(8,128)(2,1)} %reshape.1133, bf16[192,512]{1,0:T(8,128)(2,1)S(1)} %copy-done.31), kind=kOutput, calls=%fused_computation.14 | convolution fusion | flops 6660554240 | bytes 113446912 | tf_op jit(solution)/shard_map/dot_general | solution.py:167
  734.7 21.2 %fusion.7 = bf16[192,32768]{1,0:T(8,128)(2,1)} fusion(bf16[512,32768]{0,1:T(8,128)(2,1)} %get-tuple-element.59, bf16[512,192]{0,1:T(8,128)(2,1)S(1)} %copy-done), kind=kOutput, calls=%fused_computation.16 | convolution fusion | flops 6448742400 | bytes 46333952 | tf_op jit(solution)/shard_map/dot_general | solution.py:172
  755.8 30.9 %reshape.1139 = bf16[3,4,4,4,8,64,64]{6,5,4,3,2,1,0:T(8,128)(2,1)} reshape(bf16[192,32768]{1,0:T(8,128)(2,1)} %fusion.7) | data formatting | bytes 25165824 | tf_op jit(solution)/shard_map/reshape | solution.py:155
  786.7 29.0 %copy.326 = bf16[3,4,4,4,8,64,64]{6,3,5,2,1,4,0:T(4,128)(2,1)} copy(bf16[3,4,4,4,8,64,64]{6,5,4,3,2,1,0:T(8,128)(2,1)} %reshape.1139) | data formatting | bytes 25165824 | tf_op jit(solution)/shard_map/reshape | solution.py:155
  815.7 35.7 %reshape.1140 = bf16[3,32,256,256]{3,2,1,0:T(8,128)(2,1)} reshape(bf16[3,8,4,4,64,4,64]{6,5,4,3,2,1,0:T(4,128)(2,1)} %bitcast.407) | data formatting | bytes 25165824 | tf_op jit(solution)/shard_map/reshape | solution.py:158
  851.4 18.5 %fusion.44 = (bf16[1,32,256,256]{3,2,1,0:T(8,128)(2,1)}, bf16[1,32,256,256]{3,2,1,0:T(8,128)(2,1)}, bf16[1,32,256,256]{3,2,1,0:T(8,128)(2,1)}) fusion(bf16[3,32,256,256]{3,2,1,0:T(8,128)(2,1)} %reshape.1140, bf16[3,32,256,256]{3,2,1,0:T(8,128)(2,1)} %bitcast_convert_fusion.2, bf16[3,32,256,256]{3,2,1,0:T(8,128)(2,1)} %bitcast_convert_fusion.4), kind=kLoop, calls=%fused_computation.81 | loop fusion | flops 50331648 | bytes 50331648 | tf_op jit(solution)/shard_map/convert.3
  879.6 39.9 %fusion.10 = bf16[3,2,32,4,2,48,48]{6,5,2,4,0,3,1:T(8,128)(2,1)} fusion(bf16[2,2,48,3,32,256]{5,2,0,4,1,3:T(8,128)(2,1)} %fusion.22, bf16[2,256,2,4,48,1,1,1]{1,4,3,2,0,7,6,5:T(8,128)(2,1)S(1)} %bitcast.428), kind=kOutput, calls=%fused_computation.26 | convolution fusion | flops 3627417600 | bytes 16908288 | tf_op jit(solution)/shard_map/crlmxy,rysja->csxjlam/dot_general | solution.py:134
  934.9 18.2 %copy.263 = bf16[3,2,32,4,2,48,48]{6,5,2,1,0,4,3:T(8,128)(2,1)} copy(bf16[3,2,32,4,2,48,48]{6,5,2,4,0,3,1:T(8,128)(2,1)} %fusion.10) | data formatting | bytes 14155776 | tf_op jit(solution)/shard_map/reshape | solution.py:137
  953.0 26.2 %reshape.1211 = bf16[3,2,32,8,2304]{4,2,1,0,3:T(8,128)(2,1)} reshape(bf16[3,2,32,4,2,48,48]{6,5,2,1,0,4,3:T(8,128)(2,1)} %copy.263) | data formatting | bytes 14155776 | tf_op jit(solution)/shard_map/reshape | solution.py:137
  984.2 31.2 %fusion.92 = f32[192,512]{0,1:T(8,128)} fusion(bf16[192,32768]{1,0:T(8,128)(2,1)} %reshape.1133, f32[32768,512]{1,0:T(8,128)} %fusion.156, f32[512]{0:T(512)S(1)} %copy-done.32), kind=kOutput, calls=%fused_computation.154 | convolution fusion | flops 6543212544 | bytes 80087040 | tf_op jit(solution)/shard_map/dot_general | solution.py:170
  1078.5 15.5 %copy.198 = f32[3,2,2304,256]{3,2,1,0:T(8,128)} copy(f32[3,2,2304,256]{2,3,0,1:T(8,128)} %convolution_bitcast_fusion.1) | data formatting | bytes 28311552 | tf_op jit(solution)/shard_map/csxp,sxtn->ctpn/transpose | solution.py:141
  (169 shorter events, 276.3 us)
Async XLA Ops:
  7.2 651.8 %copy-start = (bf16[512,192]{0,1:T(8,128)(2,1)S(1)}, bf16[512,192]{0,1:T(8,128)(2,1)}, u32[]{:S(2)}) copy-start(bf16[512,192]{0,1:T(8,128)(2,1)} %param.7) | copy-start | bytes 589828
  8.3 12.4 %copy-start.29 = (pred[48]{0:T(512)(128)(4,1)}, pred[48]{0:T(512)(128)(4,1)S(1)}, u32[]{:S(2)}) copy-start(pred[48]{0:T(512)(128)(4,1)S(1)} %broadcast_compare_fusion) | copy-start | bytes 148
  8.9 162.3 %copy-start.20 = (f32[48]{0:T(128)}, f32[48]{0:T(128)S(1)}, u32[]{:S(2)}) copy-start(f32[48]{0:T(128)S(1)} %get-tuple-element.68) | copy-start | bytes 580
  69.9 16.6 %copy-start.17 = (pred[48,256]{1,0:T(8,128)(4,1)S(1)}, pred[48,256]{1,0:T(8,128)(4,1)}, u32[]{:S(2)}) copy-start(pred[48,256]{1,0:T(8,128)(4,1)} %copy-done.16) | copy-start | bytes 36868
  69.9 16.6 %copy-start.30 = (pred[48]{0:T(512)(128)(4,1)S(1)}, pred[48]{0:T(512)(128)(4,1)}, u32[]{:S(2)}) copy-start(pred[48]{0:T(512)(128)(4,1)} %copy-done.29) | copy-start | bytes 148
  69.9 17.0 %copy-start.28 = (f32[48]{0:T(128)S(1)}, f32[48]{0:T(128)}, u32[]{:S(2)}) copy-start(f32[48]{0:T(128)} %get-tuple-element.60) | copy-start | bytes 580
  69.9 96.3 %all-to-all-start = ((bf16[3,2,256,1,2304]{4,1,3,0,2:T(2,128)(2,1)}), bf16[3,2,256,1,2304]{4,1,3,0,2:T(2,128)(2,1)}, u32[]{:S(2)}, u32[]{:S(2)}) async-start(bf16[3,2,256,1,2304]{4,1,3,0,2:T(2,128)(2,1)} %copy.174), calls=%async_computation | async-start | bytes 14155776 | tf_op jit(solution)/shard_map/all_to_all | solution.py:106
  86.9 12.8 %copy-start.13 = (bf16[1,256,2,256]{1,3,0,2:T(8,128)(2,1)S(1)}, bf16[1,256,2,256]{1,3,0,2:T(8,128)(2,1)}, u32[]{:S(2)}) copy-start(bf16[1,256,2,256]{1,3,0,2:T(8,128)(2,1)} %copy-done.12) | copy-start | bytes 786436
  86.9 12.8 %copy-start.15 = (bf16[1,256,2,256]{1,3,0,2:T(8,128)(2,1)S(1)}, bf16[1,256,2,256]{1,3,0,2:T(8,128)(2,1)}, u32[]{:S(2)}) copy-start(bf16[1,256,2,256]{1,3,0,2:T(8,128)(2,1)} %copy-done.14) | copy-start | bytes 786436
  133.2 38.1 %copy-start.23 = (f32[48]{0:T(128)S(1)}, f32[48]{0:T(128)}, u32[]{:S(2)}) copy-start(f32[48]{0:T(128)} %get-tuple-element.69) | copy-start | bytes 580
  166.2 102.8 %all-to-all-start.1 = ((bf16[3,2,256,1,2304]{4,1,3,0,2:T(2,128)(2,1)}), bf16[3,2,256,1,2304]{4,1,3,0,2:T(2,128)(2,1)}, u32[]{:S(2)}, u32[]{:S(2)}) async-start(bf16[3,2,256,1,2304]{4,1,3,0,2:T(2,128)(2,1)} %copy.180), calls=%async_computation.1 | async-start | bytes 14155776 | tf_op jit(solution)/shard_map/all_to_all | solution.py:106
  181.0 184.1 %copy-start.10 = (bf16[2,192,2,256]{3,1,2,0:T(8,128)(2,1)}, bf16[2,192,2,256]{3,1,2,0:T(8,128)(2,1)S(1)}, u32[]{:S(2)}) copy-start(bf16[2,192,2,256]{3,1,2,0:T(8,128)(2,1)S(1)} %copy.172) | copy-start | bytes 1179652
  181.0 9.7 copy-start.26
  269.0 278.2 %all-to-all-start.2 = ((bf16[3,2,256,1,2304]{4,1,3,0,2:T(2,128)(2,1)}), bf16[3,2,256,1,2304]{4,1,3,0,2:T(2,128)(2,1)}, u32[]{:S(2)}, u32[]{:S(2)}) async-start(bf16[3,2,256,1,2304]{4,1,3,0,2:T(2,128)(2,1)} %copy.187), calls=%async_computation.2 | async-start | bytes 14155776 | tf_op jit(solution)/shard_map/all_to_all | solution.py:106
  283.7 29.0 %copy-start.18 = (bf16[2,96,256]{2,1,0:T(8,128)(2,1)S(1)}, bf16[2,96,256]{2,1,0:T(8,128)(2,1)}, u32[]{:S(2)}) copy-start(bf16[2,96,256]{2,1,0:T(8,128)(2,1)} %copy.170) | copy-start | bytes 294916
  547.3 432.0 %all-to-all-start.4 = ((bf16[3,2,32,8,2304]{4,2,1,0,3:T(8,128)(2,1)}), bf16[3,2,32,8,2304]{4,2,1,0,3:T(8,128)(2,1)}, u32[]{:S(2)}, u32[]{:S(2)}) async-start(bf16[3,2,32,8,2304]{4,2,1,0,3:T(8,128)(2,1)} %reshape.1212), calls=%async_computation.4 | async-start | bytes 14155776 | tf_op jit(solution)/shard_map/all_to_all | solution.py:138
  552.1 463.4 %reduce-scatter.10.cloned.1.call-start = ((), (), s32[]{:S(2)}) async-start(), calls=%async_computation.10 | async-start | bytes 294912
  562.0 29.2 %copy-start.11 = (bf16[2,192,2,256]{3,1,2,0:T(8,128)(2,1)S(1)}, bf16[2,192,2,256]{3,1,2,0:T(8,128)(2,1)}, u32[]{:S(2)}) copy-start(bf16[2,192,2,256]{3,1,2,0:T(8,128)(2,1)} %copy-done.10) | copy-start | bytes 1179652
  659.0 27.8 %copy-start.31 = (bf16[192,512]{1,0:T(8,128)(2,1)S(1)}, bf16[192,512]{1,0:T(8,128)(2,1)}, u32[]{:S(2)}) copy-start(bf16[192,512]{1,0:T(8,128)(2,1)} %param.9) | copy-start | bytes 589828
  659.0 27.8 %copy-start.32 = (f32[512]{0:T(512)S(1)}, f32[512]{0:T(512)}, u32[]{:S(2)}) copy-start(f32[512]{0:T(512)} %param.8) | copy-start | bytes 6148
  734.6 387.0 %reduce-scatter.6.cloned.1.call-start = ((), (), s32[]{:S(2)}) async-start(), calls=%async_computation.8 | async-start | bytes 589824 | tf_op jit(solution)/shard_map/reduce_scatter | solution.py:206
  851.4 18.6 %copy-start.19 = (bf16[2,96,256]{2,1,0:T(8,128)(2,1)S(1)}, bf16[2,96,256]{2,1,0:T(8,128)(2,1)}, u32[]{:S(2)}) copy-start(bf16[2,96,256]{2,1,0:T(8,128)(2,1)} %copy.170) | copy-start | bytes 294916
  870.0 9.6 copy-start.9
  870.0 49.5 %slice-start.4 = ((s8[12582912]{0:T(1024)(128)(4,1)}), s8[4194304]{0:T(1024)(128)(4,1)S(1)}, s32[]{:S(2)}) async-start(s8[12582912]{0:T(1024)(128)(4,1)} %bitcast.412), calls=%async_computation.15 | async-start | bytes 8388608
  870.0 49.5 %slice-start.5 = ((s8[12582912]{0:T(1024)(128)(4,1)}), s8[4194304]{0:T(1024)(128)(4,1)S(1)}, s32[]{:S(2)}) async-start(s8[12582912]{0:T(1024)(128)(4,1)} %bitcast.412), calls=%async_computation.16 | async-start | bytes 8388608
  879.6 39.9 %slice-start.6 = ((s8[12582912]{0:T(1024)(128)(4,1)}), s8[4194304]{0:T(1024)(128)(4,1)S(1)}, s32[]{:S(2)}) async-start(s8[12582912]{0:T(1024)(128)(4,1)} %bitcast.412), calls=%async_computation.17 | async-start | bytes 8388608
  979.3 88.2 %all-to-all-start.3 = ((bf16[3,2,32,8,2304]{4,2,1,0,3:T(8,128)(2,1)}), bf16[3,2,32,8,2304]{4,2,1,0,3:T(8,128)(2,1)}, u32[]{:S(2)}, u32[]{:S(2)}) async-start(bf16[3,2,32,8,2304]{4,2,1,0,3:T(8,128)(2,1)} %reshape.1211), calls=%async_computation.3 | async-start | bytes 14155776 | tf_op jit(solution)/shard_map/all_to_all | solution.py:138
  984.2 137.4 %reduce-scatter.8.cloned.1.call-start = ((), (), s32[]{:S(2)}) async-start(), calls=%async_computation.9 | async-start | bytes 589824 | tf_op jit(solution)/shard_map/reduce_scatter | solution.py:207
  1027.9 15.3 %copy-start.21 = (f32[48]{0:T(128)S(1)}, f32[48]{0:T(128)}, u32[]{:S(2)}) copy-start(f32[48]{0:T(128)} %copy-done.20) | copy-start | bytes 580
  1027.9 15.3 %copy-start.24 = (f32[48]{0:T(128)S(1)}, f32[48]{0:T(128)}, u32[]{:S(2)}) copy-start(f32[48]{0:T(128)} %get-tuple-element.69) | copy-start | bytes 580
  1027.9 15.3 %copy-start.27 = (f32[256]{0:T(256)S(1)}, f32[256]{0:T(256)}, u32[]{:S(2)}) copy-start(f32[256]{0:T(256)} %fusion.140) | copy-start | bytes 3076
  1094.0 10.3 slice-start.1
  (16 other events, 88.6 us)
Sparse Core Ops, SparseCore 0:
  734.7 35.8 reduce-scatter.9
  979.4 41.3 reduce-scatter.5
  1024.5 36.3 reduce-scatter.7
where the time goes:
time: 1150 us; the launch traced here: 1130 us
  local copies, waits for them, and re-layouts  618 us (54%)
  matrix products  297 us (26%)
  other arithmetic  115 us (10%)
  waiting for transfers between devices  46.9 us (4%)
  starting transfers between devices  36 us (3%)
  between operations  14.9 us (1%)
    reshape x4, local copies, waits for them, and re-layouts, to_boxes(): field.reshape(channels, span_x // PATCH, PATCH, PATCH, span_y // PATCH, P...  118 us
    reshape x4, local copies, waits for them, and re-layouts, to_spectral(): along_y.reshape(channels, 2, span_x, parts_x * parts_y, width_y * width_z)  88.9 us
    reshape x3, local copies, waits for them, and re-layouts, to_physical(): moved.reshape(moved.shape[0], 2, moved.shape[2], parts_x, parts_y, width_...  87.1 us
    reshape x3, local copies, waits for them, and re-layouts, to_physical(): along_x = along_x.reshape(channels, 2, length, 1, width_y * width_z)  75.2 us
    reshape x2, local copies, waits for them, and re-layouts, from_boxes(): box_values.reshape(channels, PATCH, PATCH, PATCH, span_x // PATCH, span_y...  59.9 us
    reshape x2, local copies, waits for them, and re-layouts, to_boxes(): tiles.transpose(0, 2, 3, 5, 1, 4, 6).reshape(channels * PATCH ** 3, -1)  58.2 us
    dot_general x2, matrix products, to_spectral(): jnp.einsum('crlmxy,rysja->csxjlam', along_z, y_table, preferred_element_t...  55.5 us
    dot_general x3, matrix products, to_physical(): jnp.einsum('cxtlmy,tlmz->cxyz', along_y, z_table, preferred_element_type=...  48.8 us
  transfers between devices with their start and end apart: 8, of which 2 were waited for; matrix products, arithmetic and copies ran while one was open for 85% of the time, Pallas kernels for 0%

commit v1 on v0

--- a/solution.py
+++ b/solution.py
@@ -103,7 +103,12 @@
         "crpn,rnsx->csxp", flat, inverse, preferred_element_type=jnp.float32
     ).astype(jnp.bfloat16)
     along_x = along_x.reshape(channels, 2, length, 1, width_y * width_z)
-    moved = lax.all_to_all(along_x, ("px", "py"), split_axis=2, concat_axis=3, tiled=True)
+    moved = jnp.concatenate(
+        lax.all_to_all(
+            jnp.stack(jnp.split(along_x, lax.axis_size(("px", "py")), axis=2)), ("px", "py"), 0, 0
+        ),
+        axis=3,
+    )
     blocks = moved.reshape(moved.shape[0], 2, moved.shape[2], parts_x, parts_y, width_y, width_z)
     along_y = jnp.einsum(
         "csxjlam,sjaty->cxtlmy", blocks, y_table, preferred_element_type=jnp.float32

time: 1150 us -> 1080 us (0.939)
  local copies, waits for them, and re-layouts: 618 us -> 560 us
    reshape x6 -> x0, local copies, waits for them, and re-layouts: 162 us -> none  [the longest x3 87.1 us: to_physical(): moved.reshape(moved.shape[0], 2, moved.shape[2], parts_x, parts_y, width_...]
    another operation x0 -> x6, local copies, waits for them, and re-layouts: none -> 91.2 us  [the longest x3 87.1 us: to_physical(): moved.reshape(moved.shape[0], 2, moved.shape[2], parts_x, parts_y, width_...]
    unnamed x82 -> x125, local copies, waits for them, and re-layouts: 9.59 us -> 40.4 us
    all_to_all x3 -> x0, local copies, waits for them, and re-layouts: 29.5 us -> none  [to_physical(): lax.all_to_all(along_x, ('px', 'py'), split_axis=2, concat_axis=3, tiled=...]
  transfers between devices with their start and end apart: 8 -> 8, of which waited for: 2 -> 3; matrix products, arithmetic and copies ran while one was open for 85% -> 86% of each run, Pallas kernels for 0% -> 0%
where the time goes in v1:
time: 1080 us; the launch traced here: 1060 us
  local copies, waits for them, and re-layouts  560 us (52%)
  matrix products  299 us (28%)
  other arithmetic  114 us (11%)
  waiting for transfers between devices  50.7 us (5%)
  starting transfers between devices  25.1 us (2%)
  between operations  14.7 us (1%)
    reshape x4, local copies, waits for them, and re-layouts, to_boxes(): field.reshape(channels, span_x // PATCH, PATCH, PATCH, span_y // PATCH, P...  118 us
    reshape x4, local copies, waits for them, and re-layouts, to_spectral(): along_y.reshape(channels, 2, span_x, parts_x * parts_y, width_y * width_z)  88.7 us
    another operation x3, local copies, waits for them, and re-layouts, to_physical(): moved.reshape(moved.shape[0], 2, moved.shape[2], parts_x, parts_y, width_...  87.1 us
    reshape x2, local copies, waits for them, and re-layouts, from_boxes(): box_values.reshape(channels, PATCH, PATCH, PATCH, span_x // PATCH, span_y...  59.9 us
    reshape x2, local copies, waits for them, and re-layouts, to_boxes(): tiles.transpose(0, 2, 3, 5, 1, 4, 6).reshape(channels * PATCH ** 3, -1)  58.2 us
    dot_general x2, matrix products, to_spectral(): jnp.einsum('crlmxy,rysja->csxjlam', along_z, y_table, preferred_element_t...  55.7 us
    dot_general x3, matrix products, to_physical(): jnp.einsum('cxtlmy,tlmz->cxyz', along_y, z_table, preferred_element_type=...  48.7 us
    dot_general x1, matrix products, closure_terms(): jnp.dot(w_out.T, adjoints, preferred_element_type=jnp.float32)  46.6 us
  transfers between devices with their start and end apart: 8, of which 3 were waited for; matrix products, arithmetic and copies ran while one was open for 86% of the time, Pallas kernels for 0%

profile of v1, /device:TPU:0, one launch (start us, length us, event | category | flops | bytes accessed | tf_op | source)
XLA Modules:
  0.0 1063.3 jit_solution(6464011748373633378)
XLA Ops:
  119.8 19.6 %all-to-all-done = bf16[8,3,2,32,1,2304]{5,3,1,2,4,0:T(8,128)(2,1)} async-done(((bf16[8,3,2,32,1,2304]{5,3,1,2,4,0:T(8,128)(2,1)}), bf16[8,3,2,32,1,2304]{5,3,1,2,4,0:T(8,128)(2,1)}, u32[]{:S(2)}, u32[]{:S(2)}) %all-to-all-start) | async-done | bytes 7077920 | tf_op jit(solution)/shard_map/all_to_all | solution.py:107
  177.5 29.0 %reshape_reshape.9 = bf16[3,2,32,4,2,48,48]{6,5,2,0,1,4,3:T(8,128)(2,1)} reshape(bf16[3,2,32,8,1,2304]{5,2,0,1,4,3:T(8,128)(2,1)} %bitcast.41) | data formatting | bytes 14155776 | tf_op jit(solution)/shard_map/reshape;reshape | solution.py:112
  206.4 16.9 %all-to-all-done.1 = bf16[8,3,2,32,1,2304]{5,3,1,2,4,0:T(8,128)(2,1)} async-done(((bf16[8,3,2,32,1,2304]{5,3,1,2,4,0:T(8,128)(2,1)}), bf16[8,3,2,32,1,2304]{5,3,1,2,4,0:T(8,128)(2,1)}, u32[]{:S(2)}, u32[]{:S(2)}) %all-to-all-start.1) | async-done | bytes 7077920 | tf_op jit(solution)/shard_map/all_to_all | solution.py:107
  228.4 29.0 %reshape_reshape.10 = bf16[3,2,32,4,2,48,48]{6,5,2,0,1,4,3:T(8,128)(2,1)} reshape(bf16[3,2,32,8,1,2304]{5,2,0,1,4,3:T(8,128)(2,1)} %bitcast.68) | data formatting | bytes 14155776 | tf_op jit(solution)/shard_map/reshape;reshape | solution.py:112
  257.4 16.2 %bitcast_convert_fusion.3 = bf16[3,32,256,256]{3,2,1,0:T(8,128)(2,1)} fusion(bf16[2,4,48,2,256,1,1,1]{4,2,1,3,0,7,6,5:T(8,128)(2,1)S(1)} %bitcast.515, bf16[2,2,48,256,1,1]{3,2,1,0,5,4:T(8,128)(2,1)S(1)} %bitcast.518, bf16[3,2,32,4,2,48,48]{6,5,2,0,1,4,3:T(8,128)(2,1)} %reshape_reshape.10), kind=kOutput, calls=%fused_computation.21 | convolution fusion | flops 6050807808 | bytes 20152320 | tf_op jit(solution)/shard_map/cxtlmy,tlmz->cxyz/dot_general | solution.py:116
  273.6 36.2 %reshape.1134 = bf16[3,8,4,4,64,4,64]{6,5,4,3,2,1,0:T(4,128)(2,1)} reshape(bf16[3,32,256,256]{3,2,1,0:T(8,128)(2,1)} %bitcast_convert_fusion.3) | data formatting | bytes 25165824 | tf_op jit(solution)/shard_map/reshape | solution.py:152
  309.7 16.3 %bitcast_convert_fusion.4 = bf16[3,32,256,256]{3,2,1,0:T(8,128)(2,1)} fusion(bf16[2,4,48,2,256,1,1,1]{4,2,1,3,0,7,6,5:T(8,128)(2,1)S(1)} %bitcast.516, bf16[2,2,48,256,1,1]{3,2,1,0,5,4:T(8,128)(2,1)S(1)} %bitcast.519, bf16[3,2,32,4,2,48,48]{6,5,2,0,1,4,3:T(8,128)(2,1)} %reshape_reshape.9), kind=kOutput, calls=%fused_computation.22 | convolution fusion | flops 6050807808 | bytes 20152320 | tf_op jit(solution)/shard_map/cxtlmy,tlmz->cxyz/dot_general | solution.py:116
  326.0 36.1 %reshape.1129 = bf16[3,8,4,4,64,4,64]{6,5,4,3,2,1,0:T(4,128)(2,1)} reshape(bf16[3,32,256,256]{3,2,1,0:T(8,128)(2,1)} %bitcast_convert_fusion.4) | data formatting | bytes 25165824 | tf_op jit(solution)/shard_map/reshape | solution.py:152
  380.4 15.6 %fusion.11 = bf16[3,2,32,4,2,48,48]{6,5,2,4,0,3,1:T(8,128)(2,1)} fusion(bf16[2,2,48,3,32,256]{5,2,0,4,1,3:T(8,128)(2,1)} %fusion.27, bf16[2,256,2,4,48,1,1,1]{1,4,3,2,0,7,6,5:T(8,128)(2,1)} %bitcast.513), kind=kOutput, calls=%fused_computation.27 | convolution fusion | flops 3627417600 | bytes 16908288 | tf_op jit(solution)/shard_map/crlmxy,rysja->csxjlam/dot_general | solution.py:139
  396.0 18.1 %copy.194 = bf16[3,2,32,4,2,48,48]{6,5,2,1,0,4,3:T(8,128)(2,1)} copy(bf16[3,2,32,4,2,48,48]{6,5,2,4,0,3,1:T(8,128)(2,1)} %fusion.11) | data formatting | bytes 14155776 | tf_op jit(solution)/shard_map/reshape | solution.py:142
  414.1 26.2 %reshape.1209 = bf16[3,2,32,8,2304]{4,2,1,0,3:T(8,128)(2,1)} reshape(bf16[3,2,32,4,2,48,48]{6,5,2,1,0,4,3:T(8,128)(2,1)} %copy.194) | data formatting | bytes 14155776 | tf_op jit(solution)/shard_map/reshape | solution.py:142
  440.3 22.6 %copy.248 = bf16[3,8,4,4,64,4,64]{6,4,1,5,3,2,0:T(8,128)(2,1)} copy(bf16[3,8,4,4,64,4,64]{6,5,4,3,2,1,0:T(4,128)(2,1)} %reshape.1134) | data formatting | bytes 25165824 | tf_op jit(solution)/shard_map/reshape | solution.py:152
  463.0 29.1 %reshape.1135 = bf16[192,32768]{1,0:T(8,128)(2,1)} reshape(bf16[3,4,4,4,8,64,64]{6,5,4,3,2,1,0:T(8,128)(2,1)} %bitcast.492) | data formatting | bytes 25165824 | tf_op jit(solution)/shard_map/reshape | solution.py:155
  496.9 29.1 %reshape_reshape.11 = bf16[3,2,32,4,2,48,48]{6,5,2,0,1,4,3:T(8,128)(2,1)} reshape(bf16[3,2,32,8,1,2304]{5,2,0,1,4,3:T(8,128)(2,1)} %bitcast.101) | data formatting | bytes 14155776 | tf_op jit(solution)/shard_map/reshape;reshape | solution.py:112
  526.0 16.2 %bitcast_convert_fusion.2 = bf16[3,32,256,256]{3,2,1,0:T(8,128)(2,1)} fusion(bf16[2,4,48,2,256,1,1,1]{4,2,1,3,0,7,6,5:T(8,128)(2,1)S(1)} %bitcast.517, bf16[2,2,48,256,1,1]{3,2,1,0,5,4:T(8,128)(2,1)S(1)} %bitcast.521, bf16[3,2,32,4,2,48,48]{6,5,2,0,1,4,3:T(8,128)(2,1)} %reshape_reshape.11), kind=kOutput, calls=%fused_computation.20 | convolution fusion | flops 6050807808 | bytes 20152320 | tf_op jit(solution)/shard_map/cxtlmy,tlmz->cxyz/dot_general | solution.py:116
  542.2 22.6 %copy.249 = bf16[3,8,4,4,64,4,64]{6,4,1,5,3,2,0:T(8,128)(2,1)} copy(bf16[3,8,4,4,64,4,64]{6,5,4,3,2,1,0:T(4,128)(2,1)} %reshape.1129) | data formatting | bytes 25165824 | tf_op jit(solution)/shard_map/reshape | solution.py:152
  564.8 29.1 %reshape.1130 = bf16[192,32768]{1,0:T(8,128)(2,1)} reshape(bf16[3,4,4,4,8,64,64]{6,5,4,3,2,1,0:T(8,128)(2,1)} %bitcast.493) | data formatting | bytes 25165824 | tf_op jit(solution)/shard_map/reshape | solution.py:155
  593.9 27.8 %fusion.180 = f32[32768,512]{1,0:T(8,128)} fusion(bf16[192,32768]{1,0:T(8,128)(2,1)} %reshape.1135, bf16[512,192]{0,1:T(8,128)(2,1)S(1)} %copy-done), kind=kOutput, calls=%fused_computation.308 | convolution fusion | flops 6442450944 | bytes 79888384 | tf_op jit(solution)/shard_map/dot_general | solution.py:169
  621.8 46.6 %convert_reduce_fusion = (f32[512]{0:T(512)S(1)}, bf16[512,32768]{0,1:T(8,128)(2,1)}) fusion(f32[32768,512]{1,0:T(8,128)} %fusion.180, f32[512]{0:T(512)S(1)} %copy-done.41, bf16[192,32768]{1,0:T(8,128)(2,1)} %reshape.1130, bf16[192,512]{1,0:T(8,128)(2,1)S(1)} %copy-done.40), kind=kOutput, calls=%fused_computation.14 | convolution fusion | flops 6660554240 | bytes 113446912 | tf_op jit(solution)/shard_map/dot_general | solution.py:172
  669.3 21.2 %fusion.7 = bf16[192,32768]{1,0:T(8,128)(2,1)} fusion(bf16[512,32768]{0,1:T(8,128)(2,1)} %get-tuple-element.59, bf16[512,192]{0,1:T(8,128)(2,1)S(1)} %copy-done), kind=kOutput, calls=%fused_computation.16 | convolution fusion | flops 6448742400 | bytes 46333952 | tf_op jit(solution)/shard_map/dot_general | solution.py:177
  690.6 30.9 %reshape.1136 = bf16[3,4,4,4,8,64,64]{6,5,4,3,2,1,0:T(8,128)(2,1)} reshape(bf16[192,32768]{1,0:T(8,128)(2,1)} %fusion.7) | data formatting | bytes 25165824 | tf_op jit(solution)/shard_map/reshape | solution.py:160
  721.5 29.0 %copy.247 = bf16[3,4,4,4,8,64,64]{6,3,5,2,1,4,0:T(4,128)(2,1)} copy(bf16[3,4,4,4,8,64,64]{6,5,4,3,2,1,0:T(8,128)(2,1)} %reshape.1136) | data formatting | bytes 25165824 | tf_op jit(solution)/shard_map/reshape | solution.py:160
  750.5 35.7 %reshape.1137 = bf16[3,32,256,256]{3,2,1,0:T(8,128)(2,1)} reshape(bf16[3,8,4,4,64,4,64]{6,5,4,3,2,1,0:T(4,128)(2,1)} %bitcast.494) | data formatting | bytes 25165824 | tf_op jit(solution)/shard_map/reshape | solution.py:163
  786.2 18.6 %fusion.44 = (bf16[1,32,256,256]{3,2,1,0:T(8,128)(2,1)}, bf16[1,32,256,256]{3,2,1,0:T(8,128)(2,1)}, bf16[1,32,256,256]{3,2,1,0:T(8,128)(2,1)}) fusion(bf16[3,32,256,256]{3,2,1,0:T(8,128)(2,1)} %reshape.1137, bf16[3,32,256,256]{3,2,1,0:T(8,128)(2,1)} %bitcast_convert_fusion.2, bf16[3,32,256,256]{3,2,1,0:T(8,128)(2,1)} %bitcast_convert_fusion.4), kind=kLoop, calls=%fused_computation.81 | loop fusion | flops 50331648 | bytes 50331648 | tf_op jit(solution)/shard_map/convert.3
  814.5 40.1 %fusion.10 = bf16[3,2,32,4,2,48,48]{6,5,2,4,0,3,1:T(8,128)(2,1)} fusion(bf16[2,2,48,3,32,256]{5,2,0,4,1,3:T(8,128)(2,1)} %fusion.22, bf16[2,256,2,4,48,1,1,1]{1,4,3,2,0,7,6,5:T(8,128)(2,1)S(1)} %bitcast.514), kind=kOutput, calls=%fused_computation.26 | convolution fusion | flops 3627417600 | bytes 16908288 | tf_op jit(solution)/shard_map/crlmxy,rysja->csxjlam/dot_general | solution.py:139
  854.6 15.4 %fusion.181 = f32[512,192]{1,0:T(8,128)} fusion(bf16[512,32768]{0,1:T(8,128)(2,1)} %get-tuple-element.59, bf16[192,32768]{1,0:T(8,128)(2,1)S(1)} %bitcast.500), kind=kOutput, calls=%fused_computation.309 | convolution fusion | flops 6442450944 | bytes 46530560 | tf_op jit(solution)/shard_map/dot_general | solution.py:174
  869.9 18.2 %copy.187 = bf16[3,2,32,4,2,48,48]{6,5,2,1,0,4,3:T(8,128)(2,1)} copy(bf16[3,2,32,4,2,48,48]{6,5,2,4,0,3,1:T(8,128)(2,1)} %fusion.10) | data formatting | bytes 14155776 | tf_op jit(solution)/shard_map/reshape | solution.py:142
  888.1 26.2 %reshape.1208 = bf16[3,2,32,8,2304]{4,2,1,0,3:T(8,128)(2,1)} reshape(bf16[3,2,32,4,2,48,48]{6,5,2,1,0,4,3:T(8,128)(2,1)} %copy.187) | data formatting | bytes 14155776 | tf_op jit(solution)/shard_map/reshape | solution.py:142
  919.3 31.1 %fusion.92 = f32[192,512]{0,1:T(8,128)} fusion(bf16[192,32768]{1,0:T(8,128)(2,1)} %reshape.1130, f32[32768,512]{1,0:T(8,128)} %fusion.180, f32[512]{0:T(512)S(1)} %copy-done.41), kind=kOutput, calls=%fused_computation.151 | convolution fusion | flops 6543212544 | bytes 80087040 | tf_op jit(solution)/shard_map/dot_general | solution.py:175
  962.9 15.3 %copy.129 = f32[3,2,2304,256]{3,2,1,0:T(8,128)} copy(f32[3,2,2304,256]{2,3,0,1:T(8,128)} %convolution_bitcast_fusion) | data formatting | bytes 28311552 | tf_op jit(solution)/shard_map/csxp,sxtn->ctpn/transpose | solution.py:146
  1013.6 15.4 %copy.122 = f32[3,2,2304,256]{3,2,1,0:T(8,128)} copy(f32[3,2,2304,256]{2,3,0,1:T(8,128)} %convolution_bitcast_fusion.1) | data formatting | bytes 28311552 | tf_op jit(solution)/shard_map/csxp,sxtn->ctpn/transpose | solution.py:146
  1041.7 14.8 %fusion.21 = f32[3,2,48,48,256]{4,3,2,1,0:T(8,128)} fusion(f32[3,2,48,48,256]{4,3,2,1,0:T(8,128)S(1)} %bitcast.498, f32[1,2,48,48,256]{4,3,2,1,0:T(8,128)} %maximum_bitcast_fusion.6, f32[1,2,48,48,256]{4,3,2,1,0:T(8,128)S(1)} %maximum_bitcast_fusion.5, f32[1,2,48,48,256]{4,3,2,1,0:T(8,128)} %maximum_bitcast_fusion.4, f32[48,48,256]{2,1,0:T(8,128)} %and_select_fusion, ...), kind=kLoop, calls=%fused_computation.55 | loop fusion | flops 21233664 | bytes 61341696 | tf_op jit(solution)/shard_map/add | solution.py:209
  (210 shorter events, 254.4 us)
Async XLA Ops:
  7.2 586.8 %copy-start = (bf16[512,192]{0,1:T(8,128)(2,1)S(1)}, bf16[512,192]{0,1:T(8,128)(2,1)}, u32[]{:S(2)}) copy-start(bf16[512,192]{0,1:T(8,128)(2,1)} %param.7) | copy-start | bytes 589828
  8.3 12.4 %copy-start.38 = (pred[48]{0:T(512)(128)(4,1)}, pred[48]{0:T(512)(128)(4,1)S(1)}, u32[]{:S(2)}) copy-start(pred[48]{0:T(512)(128)(4,1)S(1)} %broadcast_compare_fusion) | copy-start | bytes 148
  8.8 52.0 %copy-start.29 = (f32[48]{0:T(128)}, f32[48]{0:T(128)S(1)}, u32[]{:S(2)}) copy-start(f32[48]{0:T(128)S(1)} %get-tuple-element.68) | copy-start | bytes 580
  54.4 85.0 %all-to-all-start = ((bf16[8,3,2,32,1,2304]{5,3,1,2,4,0:T(8,128)(2,1)}), bf16[8,3,2,32,1,2304]{5,3,1,2,4,0:T(8,128)(2,1)}, u32[]{:S(2)}, u32[]{:S(2)}) async-start(bf16[8,3,2,32,1,2304]{5,3,1,2,4,0:T(8,128)(2,1)} %fusion.111), calls=%async_computation | async-start | bytes 14155776 | tf_op jit(solution)/shard_map/all_to_all | solution.py:107
  62.0 13.7 %copy-start.19 = (bf16[1,256,2,256]{1,3,0,2:T(8,128)(2,1)S(1)}, bf16[1,256,2,256]{1,3,0,2:T(8,128)(2,1)}, u32[]{:S(2)}) copy-start(bf16[1,256,2,256]{1,3,0,2:T(8,128)(2,1)} %copy-done.18) | copy-start | bytes 786436
  62.0 13.7 %copy-start.22 = (bf16[1,256,2,256]{1,3,0,2:T(8,128)(2,1)S(1)}, bf16[1,256,2,256]{1,3,0,2:T(8,128)(2,1)}, u32[]{:S(2)}) copy-start(bf16[1,256,2,256]{1,3,0,2:T(8,128)(2,1)} %copy-done.21) | copy-start | bytes 786436
  98.0 10.9 %copy-start.4 = (f32[1,1,48,48,256]{4,3,2,1,0:T(8,128)S(1)}, f32[1,1,48,48,256]{4,3,2,1,0:T(8,128)}, u32[]{:S(2)}) copy-start(f32[1,1,48,48,256]{4,3,2,1,0:T(8,128)} %get-tuple-element.27) | copy-start | bytes 7077892
  98.0 10.9 %copy-start.5 = (f32[1,1,48,48,256]{4,3,2,1,0:T(8,128)S(1)}, f32[1,1,48,48,256]{4,3,2,1,0:T(8,128)}, u32[]{:S(2)}) copy-start(f32[1,1,48,48,256]{4,3,2,1,0:T(8,128)} %get-tuple-element.28) | copy-start | bytes 7077892
  98.0 10.9 %copy-start.6 = (f32[1,1,48,48,256]{4,3,2,1,0:T(8,128)S(1)}, f32[1,1,48,48,256]{4,3,2,1,0:T(8,128)}, u32[]{:S(2)}) copy-start(f32[1,1,48,48,256]{4,3,2,1,0:T(8,128)} %get-tuple-element.29) | copy-start | bytes 7077892
  98.0 10.9 %copy-start.7 = (f32[1,1,48,48,256]{4,3,2,1,0:T(8,128)S(1)}, f32[1,1,48,48,256]{4,3,2,1,0:T(8,128)}, u32[]{:S(2)}) copy-start(f32[1,1,48,48,256]{4,3,2,1,0:T(8,128)} %get-tuple-element.30) | copy-start | bytes 7077892
  98.1 10.9 %copy-start.35 = (f32[256]{0:T(256)S(1)}, f32[256]{0:T(256)}, u32[]{:S(2)}) copy-start(f32[256]{0:T(256)} %fusion.164) | copy-start | bytes 3076
  139.4 83.9 %all-to-all-start.1 = ((bf16[8,3,2,32,1,2304]{5,3,1,2,4,0:T(8,128)(2,1)}), bf16[8,3,2,32,1,2304]{5,3,1,2,4,0:T(8,128)(2,1)}, u32[]{:S(2)}, u32[]{:S(2)}) async-start(bf16[8,3,2,32,1,2304]{5,3,1,2,4,0:T(8,128)(2,1)} %fusion.103), calls=%async_computation.1 | async-start | bytes 14155776 | tf_op jit(solution)/shard_map/all_to_all | solution.py:107
  144.2 28.2 %slice-start.7 = ((s8[7077888]{0:T(1024)(128)(4,1)}), s8[2883584]{0:T(1024)(128)(4,1)S(1)}, s32[]{:S(2)}) async-start(s8[7077888]{0:T(1024)(128)(4,1)} %bitcast.503), calls=%async_computation.18 | async-start | bytes 5767168
  163.8 146.0 %copy-start.16 = (bf16[2,192,2,256]{3,1,2,0:T(8,128)(2,1)}, bf16[2,192,2,256]{3,1,2,0:T(8,128)(2,1)S(1)}, u32[]{:S(2)}) copy-start(bf16[2,192,2,256]{3,1,2,0:T(8,128)(2,1)S(1)} %copy.102) | copy-start | bytes 1179652
  223.3 268.7 %all-to-all-start.2 = ((bf16[8,3,2,32,1,2304]{5,3,1,2,4,0:T(8,128)(2,1)}), bf16[8,3,2,32,1,2304]{5,3,1,2,4,0:T(8,128)(2,1)}, u32[]{:S(2)}, u32[]{:S(2)}) async-start(bf16[8,3,2,32,1,2304]{5,3,1,2,4,0:T(8,128)(2,1)} %fusion.95), calls=%async_computation.2 | async-start | bytes 14155776 | tf_op jit(solution)/shard_map/all_to_all | solution.py:107
  228.4 29.0 %copy-start.26 = (bf16[2,96,256]{2,1,0:T(8,128)(2,1)S(1)}, bf16[2,96,256]{2,1,0:T(8,128)(2,1)}, u32[]{:S(2)}) copy-start(bf16[2,96,256]{2,1,0:T(8,128)(2,1)} %copy.100) | copy-start | bytes 294916
  362.2 11.7 %copy-start.27 = (bf16[2,96,256]{2,1,0:T(8,128)(2,1)S(1)}, bf16[2,96,256]{2,1,0:T(8,128)(2,1)}, u32[]{:S(2)}) copy-start(bf16[2,96,256]{2,1,0:T(8,128)(2,1)} %copy.100) | copy-start | bytes 294916
  492.1 422.3 %all-to-all-start.4 = ((bf16[3,2,32,8,2304]{4,2,1,0,3:T(8,128)(2,1)}), bf16[3,2,32,8,2304]{4,2,1,0,3:T(8,128)(2,1)}, u32[]{:S(2)}, u32[]{:S(2)}) async-start(bf16[3,2,32,8,2304]{4,2,1,0,3:T(8,128)(2,1)} %reshape.1209), calls=%async_computation.4 | async-start | bytes 14155776 | tf_op jit(solution)/shard_map/all_to_all | solution.py:143
  496.8 453.6 %reduce-scatter.10.cloned.1.call-start = ((), (), s32[]{:S(2)}) async-start(), calls=%async_computation.10 | async-start | bytes 294912
  496.9 29.1 %copy-start.17 = (bf16[2,192,2,256]{3,1,2,0:T(8,128)(2,1)S(1)}, bf16[2,192,2,256]{3,1,2,0:T(8,128)(2,1)}, u32[]{:S(2)}) copy-start(bf16[2,192,2,256]{3,1,2,0:T(8,128)(2,1)} %copy-done.16) | copy-start | bytes 1179652
  593.9 27.8 %copy-start.40 = (bf16[192,512]{1,0:T(8,128)(2,1)S(1)}, bf16[192,512]{1,0:T(8,128)(2,1)}, u32[]{:S(2)}) copy-start(bf16[192,512]{1,0:T(8,128)(2,1)} %param.9) | copy-start | bytes 589828
  593.9 27.8 %copy-start.41 = (f32[512]{0:T(512)S(1)}, f32[512]{0:T(512)}, u32[]{:S(2)}) copy-start(f32[512]{0:T(512)} %param.8) | copy-start | bytes 6148
  669.3 387.2 %reduce-scatter.6.cloned.1.call-start = ((), (), s32[]{:S(2)}) async-start(), calls=%async_computation.8 | async-start | bytes 589824 | tf_op jit(solution)/shard_map/reduce_scatter | solution.py:211
  786.2 18.6 %copy-start.28 = (bf16[2,96,256]{2,1,0:T(8,128)(2,1)S(1)}, bf16[2,96,256]{2,1,0:T(8,128)(2,1)}, u32[]{:S(2)}) copy-start(bf16[2,96,256]{2,1,0:T(8,128)(2,1)} %copy.100) | copy-start | bytes 294916
  804.8 49.8 %slice-start.4 = ((s8[12582912]{0:T(1024)(128)(4,1)}), s8[4194304]{0:T(1024)(128)(4,1)S(1)}, s32[]{:S(2)}) async-start(s8[12582912]{0:T(1024)(128)(4,1)} %bitcast.499), calls=%async_computation.15 | async-start | bytes 8388608
  804.8 49.8 %slice-start.5 = ((s8[12582912]{0:T(1024)(128)(4,1)}), s8[4194304]{0:T(1024)(128)(4,1)S(1)}, s32[]{:S(2)}) async-start(s8[12582912]{0:T(1024)(128)(4,1)} %bitcast.499), calls=%async_computation.16 | async-start | bytes 8388608
  814.5 40.1 %slice-start.6 = ((s8[12582912]{0:T(1024)(128)(4,1)}), s8[4194304]{0:T(1024)(128)(4,1)S(1)}, s32[]{:S(2)}) async-start(s8[12582912]{0:T(1024)(128)(4,1)} %bitcast.499), calls=%async_computation.17 | async-start | bytes 8388608
  914.4 88.2 %all-to-all-start.3 = ((bf16[3,2,32,8,2304]{4,2,1,0,3:T(8,128)(2,1)}), bf16[3,2,32,8,2304]{4,2,1,0,3:T(8,128)(2,1)}, u32[]{:S(2)}, u32[]{:S(2)}) async-start(bf16[3,2,32,8,2304]{4,2,1,0,3:T(8,128)(2,1)} %reshape.1208), calls=%async_computation.3 | async-start | bytes 14155776 | tf_op jit(solution)/shard_map/all_to_all | solution.py:143
  919.2 137.3 %reduce-scatter.8.cloned.1.call-start = ((), (), s32[]{:S(2)}) async-start(), calls=%async_computation.9 | async-start | bytes 589824 | tf_op jit(solution)/shard_map/reduce_scatter | solution.py:212
  962.9 15.3 %copy-start.30 = (f32[48]{0:T(128)S(1)}, f32[48]{0:T(128)}, u32[]{:S(2)}) copy-start(f32[48]{0:T(128)} %copy-done.29) | copy-start | bytes 580
  962.9 15.3 %copy-start.33 = (f32[48]{0:T(128)S(1)}, f32[48]{0:T(128)}, u32[]{:S(2)}) copy-start(f32[48]{0:T(128)} %get-tuple-element.69) | copy-start | bytes 580
  962.9 15.3 %copy-start.36 = (f32[256]{0:T(256)S(1)}, f32[256]{0:T(256)}, u32[]{:S(2)}) copy-start(f32[256]{0:T(256)} %fusion.164) | copy-start | bytes 3076
  (27 other events, 155.5 us)
Sparse Core Ops, SparseCore 0:
  669.4 36.1 reduce-scatter.9
  914.5 41.5 reduce-scatter.5
  959.7 36.3 reduce-scatter.7
